TPU v7x, 256 devices: a whole 4x4x8 slice. The times are simulated.
256 devices in a mesh: row: 16 (over z, core), col: 16 (over x, y).
Axes of the slice: x: 4, y: 4, z: 8, core: 2. Of those that a mesh axis runs over, the one named last changes fastest.
Arguments:
- panel: float32 [16384, 128], P(('row', 'col')), as said below
- mobility: float32 [16384, 16384], P('row', 'col'), as said below
Outputs:
- updated: float32 [16384, 16384], P('row', 'col')
- panel_factor: float32 [128, 128], replicated
Inputs may be any that keep to these rules, and one draw needn't show every extreme that they name: Each row and each column of the panel has its own scale. `mobility`: Symmetric.
All inputs are finite; a program needn't handle non-finite values.
Results may differ from a plain program's by a relative error of at most 0.000076.
Values sent between devices are 32-bit elements; how exact they have to be, the bound alone decides.
No kernel may reach another device: no remote copies, remote signals or barrier semaphores. Data moves between devices by JAX's collectives and lax.ppermute only.
A program may use at most 64 MiB of HBM per device.

v0:
```python
import jax
import jax.numpy as jnp
from jax import lax
from jax.sharding import PartitionSpec as P


def spread(shard, axis, root):
    mine = lax.axis_index(axis) == root
    return lax.psum(jnp.where(mine, shard, jnp.zeros_like(shard)), axis)


def product(first_op, second_op):
    return jnp.dot(
        first_op, second_op, precision=lax.Precision.HIGHEST, preferred_element_type=jnp.float32
    )


def product_tn(first_op, second_op):
    return lax.dot_general(
        first_op,
        second_op,
        (((0,), (0,)), ((), ())),
        precision=lax.Precision.HIGHEST,
        preferred_element_type=jnp.float32,
    )


def product_nt(first_op, second_op):
    return lax.dot_general(
        first_op,
        second_op,
        (((1,), (1,)), ((), ())),
        precision=lax.Precision.HIGHEST,
        preferred_element_type=jnp.float32,
    )


def invert_core(core_matrix):
    identity = jnp.eye(core_matrix.shape[0], dtype=jnp.float32)

    def newton_step(index, approx):
        return product(approx, 2.0 * identity - product(core_matrix, approx))

    return lax.fori_loop(0, 12, newton_step, identity)


def correction_columns(block_rows_arr, block_ratio):
    root_index = lax.axis_index("col") * block_ratio + 0
    copies = spread(block_rows_arr, "row", root_index)
    return copies


def on_device(panel, mobility):
    piece_rows = panel.shape[0]
    width_cols = panel.shape[1]
    count_col = lax.axis_size("col")
    count_row = lax.axis_size("row")
    block_ratio = count_row // count_col
    row_index = lax.axis_index("row")
    col_index = lax.axis_index("col")
    block_rows = mobility.shape[0]
    block_cols = mobility.shape[1]
    first_row = (row_index * count_col + col_index) * piece_rows
    positions = first_row + jnp.arange(piece_rows, dtype=jnp.int32)
    selector = (jnp.arange(width_cols, dtype=jnp.int32)[:, None] == positions[None, :]).astype(
        jnp.float32
    )
    gram_term = product_tn(panel, panel)
    top_term = product(selector, panel)
    gram_sum, top_rows = lax.psum((gram_term, top_term), ("row", "col"))
    lower_factor = jnp.linalg.cholesky(gram_sum)
    panel_factor = lower_factor.T
    ortho_piece = jax.scipy.linalg.solve_triangular(lower_factor, panel.T, lower=True).T
    basis_piece = ortho_piece + selector.T
    top_ortho = jax.scipy.linalg.solve_triangular(lower_factor, top_rows.T, lower=True)
    core_matrix = jnp.eye(width_cols, dtype=jnp.float32) + top_ortho
    kernel = invert_core(core_matrix)
    everything = lax.all_gather(basis_piece, ("row", "col"), axis=0, tiled=True)
    basis_rows = lax.dynamic_slice_in_dim(everything, row_index * block_rows, block_rows, 0)
    basis_cols = lax.dynamic_slice_in_dim(everything, col_index * block_cols, block_cols, 0)
    partial_rows = product(mobility, basis_cols)
    spread_rows = product(lax.psum(partial_rows, "col"), kernel)
    inner_sum = lax.psum(product_tn(basis_rows, spread_rows), "row")
    inner = product_tn(kernel, inner_sum)
    correction_rows = spread_rows - 0.5 * product(basis_rows, inner)
    correction_cols = correction_columns(correction_rows, block_ratio)
    left_side = jnp.concatenate([basis_rows, correction_rows], axis=1)
    right_side = jnp.concatenate([correction_cols, basis_cols], axis=1)
    updated = mobility - product_nt(left_side, right_side)
    return (updated, panel_factor)


def solution(mesh):
    in_specs = (P(("row", "col"), None), P("row", "col"))
    out_specs = (P("row", "col"), P())
    return jax.shard_map(
        on_device, mesh=mesh, in_specs=in_specs, out_specs=out_specs, check_vma=False
    )
```

profile of v0, /device:TPU:1, one launch (start us, length us, event | category | flops | bytes accessed | tf_op | source)
XLA Modules:
  0.0 727.7 jit_solution(3753922273948830282)
XLA Ops:
  7.2 0.0 copy-start
  7.2 0.0 all-reduce.12.cloned.1.call-start
  7.2 0.7 copy-done
  7.9 0.9 fusion.18
  8.8 0.8 fusion.14
  9.6 0.0 all-reduce.12.cloned.1.call-update
  9.7 0.0 all-gather.2.cloned.1.call-start
  9.7 249.4 %all-reduce.12.cloned.1.call-done = (f32[128,128]{0,1:T(8,128)}, f32[128,128]{1,0:T(8,128)}) async-done(((f32[128,128]{0,1:T(8,128)}, f32[128,128]{1,0:T(8,128)}), (f32[128,128]{0,1:T(8,128)}, f32[128,128]{1,0:T(8,128)})) %all-reduce.12.cloned.1.call-update) | async-done | bytes 131088 | tf_op jit(solution)/shard_map/psum | solution.py:70
  259.1 0.9 copy.5
  260.0 0.9 fusion.12
  260.9 11.7 %cholesky.19 = f32[128,128]{1,0:T(8,128)S(1)} custom-call(f32[128,128]{1,0:T(8,128)S(1)} %fusion.12), custom_call_target="Cholesky" | custom-call | tf_op jit(solution)/shard_map/jit(cholesky)/cholesky | solution.py:71
  272.6 0.6 compare_reduce_fusion
  273.3 0.7 fusion.15
  273.9 9.8 %custom-call.10 = f32[1,128,128]{1,2,0:T(8,128)S(1)} custom-call(f32[1,128,128]{2,1,0:T(8,128)S(1)} %get-tuple-element.49), custom_call_target="InvertDiagBlocksLowerTriangular" | custom-call | tf_op jit(solution)/shard_map/jit(_solve_triangular)/triangular_solve | solution.py:73
  283.8 0.8 fusion.3
  284.6 0.0 all-gather.2.cloned.1.call-update
  284.6 0.0 all-reduce.6.cloned.1.call-start
  284.7 0.1 copy.6
  284.7 1.1 convolution_add_fusion
  285.9 115.3 %all-gather.2.cloned.1.call-done = f32[16384,128]{1,0:T(8,128)} async-done(((f32[64,128]{1,0:T(8,128)}), f32[16384,128]{1,0:T(8,128)}) %all-gather.2.cloned.1.call-update) | async-done | bytes 8388624 | tf_op jit(solution)/shard_map/all_gather | solution.py:78
  401.2 1.3 constant_dynamic-slice_fusion.1
  402.5 7.5 %convolution_bitcast_fusion.1 = f32[1024,128]{0,1:T(8,128)} fusion(f32[1024,128]{1,0:T(8,128)S(1)} %get-tuple-element.47, f32[1024,1024]{1,0:T(8,128)} %param.5), kind=kOutput, calls=%fused_computation.7 | convolution fusion | flops 1610612736 | bytes 5242880 | tf_op jit(solution)/shard_map/dot_general | solution.py:13
  409.9 0.0 all-reduce.6.cloned.1.call-update
  410.0 0.2 all-reduce.8.cloned.1.call-start
  410.2 7.1 while.11
  410.2 0.3 convolution_subtract_fusion.3
  410.5 0.3 convolution_bitcast_fusion.4
  410.8 0.3 convolution_subtract_fusion.3
  411.1 0.3 convolution_bitcast_fusion.4
  411.4 0.3 convolution_subtract_fusion.3
  411.7 0.3 convolution_bitcast_fusion.4
  412.0 0.3 convolution_subtract_fusion.3
  412.3 0.3 convolution_bitcast_fusion.4
  412.6 0.3 convolution_subtract_fusion.3
  412.9 0.3 convolution_bitcast_fusion.4
  413.2 0.3 convolution_subtract_fusion.3
  413.5 0.3 convolution_bitcast_fusion.4
  413.8 0.3 convolution_subtract_fusion.3
  414.0 0.3 convolution_bitcast_fusion.4
  414.4 0.3 convolution_subtract_fusion.3
  414.6 0.3 convolution_bitcast_fusion.4
  415.0 0.3 convolution_subtract_fusion.3
  415.2 0.3 convolution_bitcast_fusion.4
  415.6 0.3 convolution_subtract_fusion.3
  415.8 0.3 convolution_bitcast_fusion.4
  416.1 0.3 convolution_subtract_fusion.3
  416.4 0.3 convolution_bitcast_fusion.4
  416.7 0.3 convolution_subtract_fusion.3
  417.0 0.3 convolution_bitcast_fusion.4
  417.3 83.1 %all-reduce.6.cloned.1.call-done = f32[1024,128]{0,1:T(8,128)} async-done(((f32[1024,128]{0,1:T(8,128)}), f32[1024,128]{0,1:T(8,128)}) %all-reduce.6.cloned.1.call-update) | async-done | bytes 524304 | tf_op jit(solution)/shard_map/psum | solution.py:82
  500.4 1.6 fusion.19
  502.1 1.6 fusion.20
  503.7 0.0 all-reduce.8.cloned.1.call-update
  503.7 0.0 all-reduce.10.cloned.1.call-start
  503.8 0.2 copy.8
  504.0 99.9 %all-reduce.8.cloned.1.call-done = f32[128,128]{1,0:T(8,128)} async-done(((f32[128,128]{1,0:T(8,128)}), f32[128,128]{1,0:T(8,128)}) %all-reduce.8.cloned.1.call-update) | async-done | bytes 65552 | tf_op jit(solution)/shard_map/psum | solution.py:83
  603.9 1.0 fusion.21
  604.9 1.4 broadcast_select_fusion
  606.3 0.0 all-reduce.10.cloned.1.call-update
  606.3 0.7 copy.9
  607.1 107.4 %all-reduce.10.cloned.1.call-done = f32[1024,128]{1,0:T(8,128)} async-done(((f32[1024,128]{1,0:T(8,128)}), f32[1024,128]{1,0:T(8,128)}) %all-reduce.10.cloned.1.call-update) | async-done | bytes 524304 | tf_op jit(solution)/shard_map/psum | solution.py:9
  714.4 6.7 convolution_subtract_fusion.1
  (15 shorter events, 0.1 us)
Async XLA Ops:
  7.2 0.8 copy-start
  7.2 251.9 %all-reduce.12.cloned.1.call-start = ((), (), s32[]{:S(2)}) async-start(), calls=%async_computation.4 | async-start | bytes 262144 | tf_op jit(solution)/shard_map/psum | solution.py:70
  9.7 391.5 %all-gather.2.cloned.1.call-start = ((), (), s32[]{:S(2)}) async-start(), calls=%async_computation | async-start | bytes 8421376 | tf_op jit(solution)/shard_map/all_gather | solution.py:78
  284.6 215.8 %all-reduce.6.cloned.1.call-start = ((), (), s32[]{:S(2)}) async-start(), calls=%async_computation.1 | async-start | bytes 1048576 | tf_op jit(solution)/shard_map/psum | solution.py:82
  410.0 193.9 %all-reduce.8.cloned.1.call-start = ((), (), s32[]{:S(2)}) async-start(), calls=%async_computation.2 | async-start | bytes 131072 | tf_op jit(solution)/shard_map/psum | solution.py:83
  503.7 210.7 %all-reduce.10.cloned.1.call-start = ((), (), s32[]{:S(2)}) async-start(), calls=%async_computation.3 | async-start | bytes 1048576 | tf_op jit(solution)/shard_map/psum | solution.py:9
Sparse Core Ops, SparseCore 0:
  14.2 244.8 all-reduce.11
  284.7 116.4 all-gather.1
  410.1 90.2 all-reduce.5
  503.8 99.9 all-reduce.7
  606.6 107.7 all-reduce.9
where the time goes:
time: 728 us
  waiting for transfers between devices  655 us (90%)
  matrix products  30.2 us (4%)
  other arithmetic  23.7 us (3%)
  between operations  13.9 us (2%)
    psum x1, waiting for transfers between devices, on_device(): gram_sum, top_rows = lax.psum((gram_term, top_term), ('row', 'col'))  249 us
    all_gather x1, waiting for transfers between devices, on_device(): everything = lax.all_gather(basis_piece, ('row', 'col'), axis=0, tiled=True)  115 us
    psum x1, waiting for transfers between devices, spread(): return lax.psum(jnp.where(mine, shard, jnp.zeros_like(shard)), axis)  107 us
    psum x1, waiting for transfers between devices, on_device(): inner_sum = lax.psum(product_tn(basis_rows, spread_rows), 'row')  99.9 us
    psum x1, waiting for transfers between devices, on_device(): spread_rows = product(lax.psum(partial_rows, 'col'), kernel)  83.1 us
    dot_general x28, matrix products, product(): jnp.dot(first_op, second_op, precision=lax.Precision.HIGHEST, preferred_e...  17.9 us
  transfers between devices with their start and end apart: 5, of which 5 were waited for; matrix products, arithmetic and copies ran while one was open for 1% of the time, Pallas kernels for 0%

commit v1 on v0

--- a/solution.py
+++ b/solution.py
@@ -67,7 +67,7 @@
     )
     gram_term = product_tn(panel, panel)
     top_term = product(selector, panel)
-    gram_sum, top_rows = lax.psum((gram_term, top_term), ("row", "col"))
+    gram_sum, top_rows = lax.psum(lax.psum((gram_term, top_term), "col"), "row")
     lower_factor = jnp.linalg.cholesky(gram_sum)
     panel_factor = lower_factor.T
     ortho_piece = jax.scipy.linalg.solve_triangular(lower_factor, panel.T, lower=True).T

time: 728 us -> 786 us (1.080)
  waiting for transfers between devices: 655 us -> 712 us
    psum x1 -> x3, waiting for transfers between devices: 249 us -> 301 us  [on_device(): gram_sum, top_rows = lax.psum(lax.psum((gram_term, top_term), 'col'), 'row')]
  transfers between devices with their start and end apart: 5 -> 7, of which waited for: 5 -> 7; matrix products, arithmetic and copies ran while one was open for 1% -> 0% of each run, Pallas kernels for 0% -> 0%
where the time goes in v1:
time: 786 us; the launch traced here: 785 us
  waiting for transfers between devices  712 us (91%)
  matrix products  30.2 us (4%)
  other arithmetic  23.7 us (3%)
  between operations  14.2 us (2%)
    psum x3, waiting for transfers between devices, on_device(): gram_sum, top_rows = lax.psum(lax.psum((gram_term, top_term), 'col'), 'row')  301 us
    all_gather x1, waiting for transfers between devices, on_device(): everything = lax.all_gather(basis_piece, ('row', 'col'), axis=0, tiled=True)  116 us
    psum x1, waiting for transfers between devices, spread(): return lax.psum(jnp.where(mine, shard, jnp.zeros_like(shard)), axis)  108 us
    psum x1, waiting for transfers between devices, on_device(): inner_sum = lax.psum(product_tn(basis_rows, spread_rows), 'row')  97.3 us
    psum x1, waiting for transfers between devices, on_device(): spread_rows = product(lax.psum(partial_rows, 'col'), kernel)  90.4 us
    dot_general x28, matrix products, product(): jnp.dot(first_op, second_op, precision=lax.Precision.HIGHEST, preferred_e...  17.9 us
  transfers between devices with their start and end apart: 7, of which 7 were waited for; matrix products, arithmetic and copies ran while one was open for 0% of the time, Pallas kernels for 0%

profile of v1, /device:TPU:1, one launch (start us, length us, event | category | flops | bytes accessed | tf_op | source)
XLA Modules:
  0.0 785.3 jit_solution(9439968328560815604)
XLA Ops:
  7.2 0.0 all-reduce.8.cloned.1.call-start
  7.2 0.7 copy-done
  7.9 0.9 fusion.18
  8.9 0.0 all-reduce.10.cloned.1.call-start
  8.9 96.2 %all-reduce.8.cloned.1.call-done = f32[128,128]{0,1:T(8,128)} async-done(((f32[128,128]{0,1:T(8,128)}), f32[128,128]{0,1:T(8,128)}) %all-reduce.8.cloned.1.call-update) | async-done | bytes 65552 | tf_op jit(solution)/shard_map/psum | solution.py:70
  105.1 0.0 all-reduce.10.cloned.1.call-update
  105.2 0.0 all-gather.2.cloned.1.call-start
  105.2 102.7 %all-reduce.10.cloned.1.call-done = f32[128,128]{0,1:T(8,128)} async-done(((f32[128,128]{0,1:T(8,128)}), f32[128,128]{0,1:T(8,128)}) %all-reduce.10.cloned.1.call-update) | async-done | bytes 65552 | tf_op jit(solution)/shard_map/psum | solution.py:70
  207.9 0.9 copy.5
  208.8 0.9 fusion.12
  209.7 11.7 %cholesky.19 = f32[128,128]{1,0:T(8,128)S(1)} custom-call(f32[128,128]{1,0:T(8,128)S(1)} %fusion.12), custom_call_target="Cholesky" | custom-call | tf_op jit(solution)/shard_map/jit(cholesky)/cholesky | solution.py:71
  221.4 0.6 compare_reduce_fusion
  222.1 0.7 fusion.15
  222.7 9.8 %custom-call.10 = f32[1,128,128]{1,2,0:T(8,128)S(1)} custom-call(f32[1,128,128]{2,1,0:T(8,128)S(1)} %get-tuple-element.49), custom_call_target="InvertDiagBlocksLowerTriangular" | custom-call | tf_op jit(solution)/shard_map/jit(_solve_triangular)/triangular_solve | solution.py:73
  232.5 0.8 fusion.3
  233.3 0.0 all-gather.2.cloned.1.call-update
  233.4 0.0 all-reduce.18.cloned.1.call-start
  233.4 0.8 fusion.14
  234.2 116.2 %all-gather.2.cloned.1.call-done = f32[16384,128]{1,0:T(8,128)} async-done(((f32[64,128]{1,0:T(8,128)}), f32[16384,128]{1,0:T(8,128)}) %all-gather.2.cloned.1.call-update) | async-done | bytes 8388624 | tf_op jit(solution)/shard_map/all_gather | solution.py:78
  350.4 1.3 constant_dynamic-slice_fusion.1
  351.7 7.5 convolution_bitcast_fusion.1
  359.1 0.0 all-reduce.18.cloned.1.call-update
  359.1 0.0 all-reduce.12.cloned.1.call-start
  359.2 90.4 %all-reduce.18.cloned.1.call-done = (f32[1024,128]{0,1:T(8,128)}, f32[128,128]{1,0:T(8,128)}) async-done(((f32[1024,128]{0,1:T(8,128)}, f32[128,128]{1,0:T(8,128)}), (f32[1024,128]{0,1:T(8,128)}, f32[128,128]{1,0:T(8,128)})) %all-reduce.18.cloned.1.call-update) | async-done | bytes 589840 | tf_op jit(solution)/shard_map/psum | solution.py:82
  449.6 0.0 all-reduce.12.cloned.1.call-update
  449.7 0.2 all-reduce.14.cloned.1.call-start
  449.9 0.1 copy.6
  450.0 101.9 %all-reduce.12.cloned.1.call-done = f32[128,128]{1,0:T(8,128)} async-done(((f32[128,128]{1,0:T(8,128)}), f32[128,128]{1,0:T(8,128)}) %all-reduce.12.cloned.1.call-update) | async-done | bytes 65552 | tf_op jit(solution)/shard_map/psum | solution.py:70
  551.9 1.1 convolution_add_fusion
  553.0 7.1 while.11
  553.0 0.3 convolution_subtract_fusion.3
  553.3 0.3 convolution_bitcast_fusion.4
  553.6 0.3 convolution_subtract_fusion.3
  553.9 0.3 convolution_bitcast_fusion.4
  554.2 0.3 convolution_subtract_fusion.3
  554.5 0.3 convolution_bitcast_fusion.4
  554.8 0.3 convolution_subtract_fusion.3
  555.1 0.3 convolution_bitcast_fusion.4
  555.4 0.3 convolution_subtract_fusion.3
  555.7 0.3 convolution_bitcast_fusion.4
  556.0 0.3 convolution_subtract_fusion.3
  556.3 0.3 convolution_bitcast_fusion.4
  556.6 0.3 convolution_subtract_fusion.3
  556.9 0.3 convolution_bitcast_fusion.4
  557.2 0.3 convolution_subtract_fusion.3
  557.4 0.3 convolution_bitcast_fusion.4
  557.8 0.3 convolution_subtract_fusion.3
  558.0 0.3 convolution_bitcast_fusion.4
  558.4 0.3 convolution_subtract_fusion.3
  558.6 0.3 convolution_bitcast_fusion.4
  559.0 0.3 convolution_subtract_fusion.3
  559.2 0.3 convolution_bitcast_fusion.4
  559.5 0.3 convolution_subtract_fusion.3
  559.8 0.3 convolution_bitcast_fusion.4
  560.1 1.6 fusion.19
  561.8 1.6 fusion.20
  563.4 0.0 all-reduce.16.cloned.1.call-start
  563.5 0.2 copy.8
  563.7 97.3 %all-reduce.14.cloned.1.call-done = f32[128,128]{1,0:T(8,128)} async-done(((f32[128,128]{1,0:T(8,128)}), f32[128,128]{1,0:T(8,128)}) %all-reduce.14.cloned.1.call-update) | async-done | bytes 65552 | tf_op jit(solution)/shard_map/psum | solution.py:83
  661.0 1.0 fusion.21
  662.1 1.4 broadcast_select_fusion
  663.4 0.7 copy.9
  664.2 107.5 %all-reduce.16.cloned.1.call-done = f32[1024,128]{1,0:T(8,128)} async-done(((f32[1024,128]{1,0:T(8,128)}), f32[1024,128]{1,0:T(8,128)}) %all-reduce.16.cloned.1.call-update) | async-done | bytes 524304 | tf_op jit(solution)/shard_map/psum | solution.py:9
  771.7 6.8 convolution_subtract_fusion.1
  (19 shorter events, 0.2 us)
Async XLA Ops:
  7.2 0.8 copy-start
  7.2 98.0 %all-reduce.8.cloned.1.call-start = ((), (), s32[]{:S(2)}) async-start(), calls=%async_computation | async-start | bytes 131072 | tf_op jit(solution)/shard_map/psum | solution.py:70
  8.9 199.0 %all-reduce.10.cloned.1.call-start = ((), (), s32[]{:S(2)}) async-start(), calls=%async_computation.1 | async-start | bytes 131072 | tf_op jit(solution)/shard_map/psum | solution.py:70
  105.2 245.2 %all-gather.2.cloned.1.call-start = ((), (), s32[]{:S(2)}) async-start(), calls=%async_computation.2 | async-start | bytes 8421376 | tf_op jit(solution)/shard_map/all_gather | solution.py:78
  233.4 216.3 %all-reduce.18.cloned.1.call-start = ((), (), s32[]{:S(2)}) async-start(), calls=%async_computation.6 | async-start | bytes 1179648 | tf_op jit(solution)/shard_map/psum | solution.py:82
  359.1 192.7 %all-reduce.12.cloned.1.call-start = ((), (), s32[]{:S(2)}) async-start(), calls=%async_computation.3 | async-start | bytes 131072 | tf_op jit(solution)/shard_map/psum | solution.py:70
  449.7 211.3 %all-reduce.14.cloned.1.call-start = ((), (), s32[]{:S(2)}) async-start(), calls=%async_computation.4 | async-start | bytes 131072 | tf_op jit(solution)/shard_map/psum | solution.py:83
  563.4 208.3 %all-reduce.16.cloned.1.call-start = ((), (), s32[]{:S(2)}) async-start(), calls=%async_computation.5 | async-start | bytes 1048576 | tf_op jit(solution)/shard_map/psum | solution.py:9
Sparse Core Ops, SparseCore 0:
  11.8 93.3 all-reduce.7
  107.6 100.2 all-reduce.9
  233.5 116.8 all-gather.1
  359.3 90.3 all-reduce.17
  451.8 100.0 all-reduce.11
  563.5 97.4 all-reduce.13
  663.9 107.7 all-reduce.15
